TPU v7x, 32 devices: a whole 2x2x4 slice. The times are simulated.
32 devices in a mesh: gx: 16 (over z, y, x), gz: 2 (over core).
Axes of the slice: x: 2, y: 2, z: 4, core: 2. Of those that a mesh axis runs over, the one named last changes fastest.
Arguments:
- modes: bfloat16 [2, 192, 96, 3, 128], P(None, 'gx', 'gz'), may hold values from -6 to 6
- wall_grad: bfloat16 [2, 192, 96, 3, 128], P(None, 'gx', 'gz'), may hold values from -6 to 6
Outputs:
- convective: float32 [128, 128, 128], P('gx', 'gz')
All inputs are finite; a program needn't handle non-finite values.
Results may differ from a plain program's by a relative error of at most 0.0038.
Values may be sent and summed in bfloat16 or wider, within the bound.
No kernel may reach another device: no remote copies, remote signals or barrier semaphores. Data moves between devices by JAX's collectives and lax.ppermute only.
A program may use at most 64 MiB of HBM per device.

v0:
```python
import math

import jax
import jax.numpy as jnp
from jax import lax
from jax.sharding import PartitionSpec as P

M = 128


def padded_2(block, sides, width):
    for axis, dim in sides:
        count = lax.axis_size(axis)
        forward = [(i, i + 1) for i in range(count - 1)]
        forward.append((count - 1, 0))
        backward = [(target, source) for source, target in forward]
        low = lax.ppermute(
            lax.slice_in_dim(block, block.shape[dim] - width, None, axis=dim), axis, forward
        )
        high = lax.ppermute(lax.slice_in_dim(block, 0, width, axis=dim), axis, backward)
        block = jnp.concatenate([low, block, high], axis=dim)
    return block


def derive_local(padded, axis, cells_x, cells_z):
    coefs = (0.75, -0.15, 1.0 / 60.0)
    total = jnp.zeros(padded[:, 3 : 3 + cells_x, 3 : 3 + cells_z].shape, jnp.float32)
    for shift_by, coef in zip((1, 2, 3), coefs):
        if axis == 1:
            upper = padded[:, 3 + shift_by : 3 + shift_by + cells_x, 3 : 3 + cells_z]
            lower = padded[:, 3 - shift_by : 3 - shift_by + cells_x, 3 : 3 + cells_z]
        else:
            upper = padded[:, 3 : 3 + cells_x, 3 + shift_by : 3 + shift_by + cells_z]
            lower = padded[:, 3 : 3 + cells_x, 3 - shift_by : 3 - shift_by + cells_z]
        total = total + coef * (upper - lower)
    return total


def per_device(modes, wall_grad):
    planes, cells_x, cells_z = (modes.shape[0], modes.shape[1], modes.shape[2])
    count_x = lax.axis_size("gx")
    count_z = lax.axis_size("gz")
    weight = 1.0 / math.sqrt(planes * cells_x * cells_z * count_x * count_z)
    padded = padded_2(modes, (("gx", 1), ("gz", 2)), 3).astype(jnp.float32)
    points = planes * cells_x * cells_z
    grad_x = derive_local(padded, 1, cells_x, cells_z).astype(jnp.bfloat16).reshape(points, 3, M)
    grad_z = derive_local(padded, 2, cells_x, cells_z).astype(jnp.bfloat16).reshape(points, 3, M)
    grad_y = wall_grad.reshape(points, 3, M)
    flat = modes.reshape(points, 3, M)
    left = flat.reshape(points * 3, M)
    grads = (grad_x, grad_y, grad_z)

    def block_term(k_start, k_count):
        adv = jnp.zeros((points, 3, k_count, M), jnp.float32)
        for comp in range(3):
            part = lax.dynamic_slice_in_dim(grads[comp], k_start, k_count, 2)
            adv = adv + part[:, :, :, None].astype(jnp.float32) * flat[
                :, comp, None, None, :
            ].astype(jnp.float32)
        adv = adv.astype(jnp.bfloat16).reshape(points * 3, k_count * M)
        prod = lax.dot_general(
            left, adv, (((0,), (0,)), ((), ())), preferred_element_type=jnp.float32
        )
        return prod.reshape(M, k_count, M) * weight

    step_size = math.gcd(M, 8)

    def one(index):
        term = block_term(0 + index * step_size, step_size)
        return jnp.transpose(term, (1, 0, 2))

    pieces = lax.map(one, jnp.arange(M // step_size, dtype=jnp.int32))
    whole = jnp.transpose(pieces.reshape(M, M, M), (1, 0, 2))
    slab = lax.psum_scatter(whole, "gz", scatter_dimension=0, tiled=True)
    owned = lax.psum_scatter(slab, "gx", scatter_dimension=1, tiled=True)
    result = jnp.transpose(owned, (1, 0, 2))
    return result


def solution(mesh):
    placed = (P(None, "gx", "gz", None, None), P(None, "gx", "gz", None, None))
    return jax.shard_map(
        per_device, mesh=mesh, in_specs=placed, out_specs=P("gx", "gz", None), check_vma=False
    )
```

profile of v0, /device:TPU:0, one launch (start us, length us, event | category | flops | bytes accessed | tf_op | source)
XLA Modules:
  0.0 521.7 jit_solution(14372060729974456045)
XLA Ops:
  7.7 3.0 collective-permute-start
  10.7 4.1 collective-permute-start.1
  14.8 5.5 %collective-permute-done = bf16[2,3,48,3,128]{4,2,3,1,0:T(8,128)(2,1)S(1)} collective-permute-done((bf16[2,3,48,3,128]{4,2,3,1,0:T(8,128)(2,1)S(1)}, bf16[2,3,48,3,128]{4,2,3,1,0:T(8,128)(2,1)S(1)}, u32[]{:S(2)}, u32[]{:S(2)}) %collective-permute-start) | collective-permute-done | bytes 221216 | tf_op jit(solution)/shard_map/ppermute | solution.py:17
  28.4 2.6 fusion.8
  34.3 364.8 %while.10 = (s32[]{:T(128)}, f32[16,8,128,128]{3,2,1,0:T(8,128)}, s32[16]{0:T(128)S(1)}, bf16[1152,3,128]{2,1,0:T(4,128)(2,1)}, bf16[1152,3,128]{2,1,0:T(4,128)(...) while((s32[]{:T(128)}, f32[16,8,128,128]{3,2,1,0:T(8,128)}, ...), condition=%wide.region_1.2_spmd, body=%wide.region_0.1_spmd.sunk | while | flops 927859712 | bytes 26454740 | solution.py:72
  41.1 12.9 %add_convert_fusion.2 = bf16[1152,3,8,128]{3,2,1,0:T(8,128)(2,1)S(1)} fusion(f32[1152,128]{1,0:T(8,128)S(1)} %bitcast.46, f32[1152,3,8]{2,1,0:T(4,128)S(1)} %get-tuple-element.130, f32[1152,128]{1,0:T(8,128)S(1)} %bitcast.47, f32[1152,3,8]{2,1,0:T(4,128)S(1)} %get-tuple-element.132, f32[1152,128]{1,0:T(8,128)S(1)} %bitcast.45, ...), kind=kLoop, calls=%fused_computation.clone.1 | loop fusion | flops 21233664 | bytes 9179136 | tf_op jit(solution)/shard_map/while/body/eval_jaxpr/convert_element_type | solution.py:60
  58.3 2.5 dynamic-slice_convert_fusion.5
  63.9 12.9 %add_convert_fusion.2 = bf16[1152,3,8,128]{3,2,1,0:T(8,128)(2,1)S(1)} fusion(f32[1152,128]{1,0:T(8,128)S(1)} %bitcast.46, f32[1152,3,8]{2,1,0:T(4,128)S(1)} %get-tuple-element.130, f32[1152,128]{1,0:T(8,128)S(1)} %bitcast.47, f32[1152,3,8]{2,1,0:T(4,128)S(1)} %get-tuple-element.132, f32[1152,128]{1,0:T(8,128)S(1)} %bitcast.45, ...), kind=kLoop, calls=%fused_computation.clone.1 | loop fusion | flops 21233664 | bytes 9179136 | tf_op jit(solution)/shard_map/while/body/eval_jaxpr/convert_element_type | solution.py:60
  86.7 12.9 %add_convert_fusion.2 = bf16[1152,3,8,128]{3,2,1,0:T(8,128)(2,1)S(1)} fusion(f32[1152,128]{1,0:T(8,128)S(1)} %bitcast.46, f32[1152,3,8]{2,1,0:T(4,128)S(1)} %get-tuple-element.130, f32[1152,128]{1,0:T(8,128)S(1)} %bitcast.47, f32[1152,3,8]{2,1,0:T(4,128)S(1)} %get-tuple-element.132, f32[1152,128]{1,0:T(8,128)S(1)} %bitcast.45, ...), kind=kLoop, calls=%fused_computation.clone.1 | loop fusion | flops 21233664 | bytes 9179136 | tf_op jit(solution)/shard_map/while/body/eval_jaxpr/convert_element_type | solution.py:60
  109.5 12.9 %add_convert_fusion.2 = bf16[1152,3,8,128]{3,2,1,0:T(8,128)(2,1)S(1)} fusion(f32[1152,128]{1,0:T(8,128)S(1)} %bitcast.46, f32[1152,3,8]{2,1,0:T(4,128)S(1)} %get-tuple-element.130, f32[1152,128]{1,0:T(8,128)S(1)} %bitcast.47, f32[1152,3,8]{2,1,0:T(4,128)S(1)} %get-tuple-element.132, f32[1152,128]{1,0:T(8,128)S(1)} %bitcast.45, ...), kind=kLoop, calls=%fused_computation.clone.1 | loop fusion | flops 21233664 | bytes 9179136 | tf_op jit(solution)/shard_map/while/body/eval_jaxpr/convert_element_type | solution.py:60
  132.3 12.9 %add_convert_fusion.2 = bf16[1152,3,8,128]{3,2,1,0:T(8,128)(2,1)S(1)} fusion(f32[1152,128]{1,0:T(8,128)S(1)} %bitcast.46, f32[1152,3,8]{2,1,0:T(4,128)S(1)} %get-tuple-element.130, f32[1152,128]{1,0:T(8,128)S(1)} %bitcast.47, f32[1152,3,8]{2,1,0:T(4,128)S(1)} %get-tuple-element.132, f32[1152,128]{1,0:T(8,128)S(1)} %bitcast.45, ...), kind=kLoop, calls=%fused_computation.clone.1 | loop fusion | flops 21233664 | bytes 9179136 | tf_op jit(solution)/shard_map/while/body/eval_jaxpr/convert_element_type | solution.py:60
  155.1 12.9 %add_convert_fusion.2 = bf16[1152,3,8,128]{3,2,1,0:T(8,128)(2,1)S(1)} fusion(f32[1152,128]{1,0:T(8,128)S(1)} %bitcast.46, f32[1152,3,8]{2,1,0:T(4,128)S(1)} %get-tuple-element.130, f32[1152,128]{1,0:T(8,128)S(1)} %bitcast.47, f32[1152,3,8]{2,1,0:T(4,128)S(1)} %get-tuple-element.132, f32[1152,128]{1,0:T(8,128)S(1)} %bitcast.45, ...), kind=kLoop, calls=%fused_computation.clone.1 | loop fusion | flops 21233664 | bytes 9179136 | tf_op jit(solution)/shard_map/while/body/eval_jaxpr/convert_element_type | solution.py:60
  177.9 12.9 %add_convert_fusion.2 = bf16[1152,3,8,128]{3,2,1,0:T(8,128)(2,1)S(1)} fusion(f32[1152,128]{1,0:T(8,128)S(1)} %bitcast.46, f32[1152,3,8]{2,1,0:T(4,128)S(1)} %get-tuple-element.130, f32[1152,128]{1,0:T(8,128)S(1)} %bitcast.47, f32[1152,3,8]{2,1,0:T(4,128)S(1)} %get-tuple-element.132, f32[1152,128]{1,0:T(8,128)S(1)} %bitcast.45, ...), kind=kLoop, calls=%fused_computation.clone.1 | loop fusion | flops 21233664 | bytes 9179136 | tf_op jit(solution)/shard_map/while/body/eval_jaxpr/convert_element_type | solution.py:60
  200.7 12.9 %add_convert_fusion.2 = bf16[1152,3,8,128]{3,2,1,0:T(8,128)(2,1)S(1)} fusion(f32[1152,128]{1,0:T(8,128)S(1)} %bitcast.46, f32[1152,3,8]{2,1,0:T(4,128)S(1)} %get-tuple-element.130, f32[1152,128]{1,0:T(8,128)S(1)} %bitcast.47, f32[1152,3,8]{2,1,0:T(4,128)S(1)} %get-tuple-element.132, f32[1152,128]{1,0:T(8,128)S(1)} %bitcast.45, ...), kind=kLoop, calls=%fused_computation.clone.1 | loop fusion | flops 21233664 | bytes 9179136 | tf_op jit(solution)/shard_map/while/body/eval_jaxpr/convert_element_type | solution.py:60
  223.5 12.9 %add_convert_fusion.2 = bf16[1152,3,8,128]{3,2,1,0:T(8,128)(2,1)S(1)} fusion(f32[1152,128]{1,0:T(8,128)S(1)} %bitcast.46, f32[1152,3,8]{2,1,0:T(4,128)S(1)} %get-tuple-element.130, f32[1152,128]{1,0:T(8,128)S(1)} %bitcast.47, f32[1152,3,8]{2,1,0:T(4,128)S(1)} %get-tuple-element.132, f32[1152,128]{1,0:T(8,128)S(1)} %bitcast.45, ...), kind=kLoop, calls=%fused_computation.clone.1 | loop fusion | flops 21233664 | bytes 9179136 | tf_op jit(solution)/shard_map/while/body/eval_jaxpr/convert_element_type | solution.py:60
  246.3 12.9 %add_convert_fusion.2 = bf16[1152,3,8,128]{3,2,1,0:T(8,128)(2,1)S(1)} fusion(f32[1152,128]{1,0:T(8,128)S(1)} %bitcast.46, f32[1152,3,8]{2,1,0:T(4,128)S(1)} %get-tuple-element.130, f32[1152,128]{1,0:T(8,128)S(1)} %bitcast.47, f32[1152,3,8]{2,1,0:T(4,128)S(1)} %get-tuple-element.132, f32[1152,128]{1,0:T(8,128)S(1)} %bitcast.45, ...), kind=kLoop, calls=%fused_computation.clone.1 | loop fusion | flops 21233664 | bytes 9179136 | tf_op jit(solution)/shard_map/while/body/eval_jaxpr/convert_element_type | solution.py:60
  269.1 12.9 %add_convert_fusion.2 = bf16[1152,3,8,128]{3,2,1,0:T(8,128)(2,1)S(1)} fusion(f32[1152,128]{1,0:T(8,128)S(1)} %bitcast.46, f32[1152,3,8]{2,1,0:T(4,128)S(1)} %get-tuple-element.130, f32[1152,128]{1,0:T(8,128)S(1)} %bitcast.47, f32[1152,3,8]{2,1,0:T(4,128)S(1)} %get-tuple-element.132, f32[1152,128]{1,0:T(8,128)S(1)} %bitcast.45, ...), kind=kLoop, calls=%fused_computation.clone.1 | loop fusion | flops 21233664 | bytes 9179136 | tf_op jit(solution)/shard_map/while/body/eval_jaxpr/convert_element_type | solution.py:60
  291.9 12.9 %add_convert_fusion.2 = bf16[1152,3,8,128]{3,2,1,0:T(8,128)(2,1)S(1)} fusion(f32[1152,128]{1,0:T(8,128)S(1)} %bitcast.46, f32[1152,3,8]{2,1,0:T(4,128)S(1)} %get-tuple-element.130, f32[1152,128]{1,0:T(8,128)S(1)} %bitcast.47, f32[1152,3,8]{2,1,0:T(4,128)S(1)} %get-tuple-element.132, f32[1152,128]{1,0:T(8,128)S(1)} %bitcast.45, ...), kind=kLoop, calls=%fused_computation.clone.1 | loop fusion | flops 21233664 | bytes 9179136 | tf_op jit(solution)/shard_map/while/body/eval_jaxpr/convert_element_type | solution.py:60
  314.7 12.9 %add_convert_fusion.2 = bf16[1152,3,8,128]{3,2,1,0:T(8,128)(2,1)S(1)} fusion(f32[1152,128]{1,0:T(8,128)S(1)} %bitcast.46, f32[1152,3,8]{2,1,0:T(4,128)S(1)} %get-tuple-element.130, f32[1152,128]{1,0:T(8,128)S(1)} %bitcast.47, f32[1152,3,8]{2,1,0:T(4,128)S(1)} %get-tuple-element.132, f32[1152,128]{1,0:T(8,128)S(1)} %bitcast.45, ...), kind=kLoop, calls=%fused_computation.clone.1 | loop fusion | flops 21233664 | bytes 9179136 | tf_op jit(solution)/shard_map/while/body/eval_jaxpr/convert_element_type | solution.py:60
  337.5 12.9 %add_convert_fusion.2 = bf16[1152,3,8,128]{3,2,1,0:T(8,128)(2,1)S(1)} fusion(f32[1152,128]{1,0:T(8,128)S(1)} %bitcast.46, f32[1152,3,8]{2,1,0:T(4,128)S(1)} %get-tuple-element.130, f32[1152,128]{1,0:T(8,128)S(1)} %bitcast.47, f32[1152,3,8]{2,1,0:T(4,128)S(1)} %get-tuple-element.132, f32[1152,128]{1,0:T(8,128)S(1)} %bitcast.45, ...), kind=kLoop, calls=%fused_computation.clone.1 | loop fusion | flops 21233664 | bytes 9179136 | tf_op jit(solution)/shard_map/while/body/eval_jaxpr/convert_element_type | solution.py:60
  360.3 12.9 %add_convert_fusion.2 = bf16[1152,3,8,128]{3,2,1,0:T(8,128)(2,1)S(1)} fusion(f32[1152,128]{1,0:T(8,128)S(1)} %bitcast.46, f32[1152,3,8]{2,1,0:T(4,128)S(1)} %get-tuple-element.130, f32[1152,128]{1,0:T(8,128)S(1)} %bitcast.47, f32[1152,3,8]{2,1,0:T(4,128)S(1)} %get-tuple-element.132, f32[1152,128]{1,0:T(8,128)S(1)} %bitcast.45, ...), kind=kLoop, calls=%fused_computation.clone.1 | loop fusion | flops 21233664 | bytes 9179136 | tf_op jit(solution)/shard_map/while/body/eval_jaxpr/convert_element_type | solution.py:60
  383.1 12.9 %add_convert_fusion.2 = bf16[1152,3,8,128]{3,2,1,0:T(8,128)(2,1)S(1)} fusion(f32[1152,128]{1,0:T(8,128)S(1)} %bitcast.46, f32[1152,3,8]{2,1,0:T(4,128)S(1)} %get-tuple-element.130, f32[1152,128]{1,0:T(8,128)S(1)} %bitcast.47, f32[1152,3,8]{2,1,0:T(4,128)S(1)} %get-tuple-element.132, f32[1152,128]{1,0:T(8,128)S(1)} %bitcast.45, ...), kind=kLoop, calls=%fused_computation.clone.1 | loop fusion | flops 21233664 | bytes 9179136 | tf_op jit(solution)/shard_map/while/body/eval_jaxpr/convert_element_type | solution.py:60
  399.2 16.8 %reduce-scatter.3.cloned.1.call-done = f32[64,128,128]{2,0,1:T(8,128)} async-done(((f32[128,128,128]{2,0,1:T(8,128)}), f32[64,128,128]{2,0,1:T(8,128)}) %reduce-scatter.3.cloned.1.call-update) | async-done | bytes 4194320 | tf_op jit(solution)/shard_map/reduce_scatter | solution.py:74
  416.0 98.8 %reduce-scatter.5.cloned.1.call-done = f32[64,8,128]{2,0,1:T(8,128)} async-done(((f32[64,128,128]{2,0,1:T(8,128)}), f32[64,8,128]{2,0,1:T(8,128)}) %reduce-scatter.5.cloned.1.call-update) | async-done | bytes 262160 | tf_op jit(solution)/shard_map/reduce_scatter | solution.py:75
  (171 shorter events, 158.5 us)
Async XLA Ops:
  6.5 13.7 %copy-start = (bf16[2,12,48,3,128]{4,2,3,1,0:T(8,128)(2,1)S(1)}, bf16[2,12,48,3,128]{4,2,3,1,0:T(8,128)(2,1)}, u32[]{:S(2)}) copy-start(bf16[2,12,48,3,128]{4,2,3,1,0:T(8,128)(2,1)} %param.4) | copy-start | bytes 2654212
  6.5 409.5 %reduce-scatter.3.cloned.1.call-start = ((), (), s32[]{:S(2)}) async-start(), calls=%async_computation.2 | async-start | bytes 12582912 | tf_op jit(solution)/shard_map/reduce_scatter | solution.py:74
  7.7 12.5 %collective-permute-start = (bf16[2,3,48,3,128]{4,2,3,1,0:T(8,128)(2,1)S(1)}, bf16[2,3,48,3,128]{4,2,3,1,0:T(8,128)(2,1)S(1)}, u32[]{:S(2)}, u32[]{:S(2)}) collective-permute-start(bf16[2,3,48,3,128]{4,2,3,1,0:T(8,128)(2,1)S(1)} %get-tuple-element.74), channel_id=1, source_target_pairs={{0,2},{2,4},{4,6},{6,8},{8,10},{10,12},{12,14},{14,16},{16,18},{18... | collective-permute-start | bytes 663560 | tf_op jit(solution)/shard_map/ppermute | solution.py:17
  10.7 11.4 %collective-permute-start.1 = (bf16[2,3,48,3,128]{4,2,3,1,0:T(8,128)(2,1)S(1)}, bf16[2,3,48,3,128]{4,2,3,1,0:T(8,128)(2,1)S(1)}, u32[]{:S(2)}, u32[]{:S(2)}) collective-permute-start(bf16[2,3,48,3,128]{4,2,3,1,0:T(8,128)(2,1)S(1)} %get-tuple-element.73), channel_id=1, source_target_pairs={{2,0},{4,2},{6,4},{8,6},{10,8},{12,10},{14,12},{16,14},{18,16},{20... | collective-permute-start | bytes 663560 | tf_op jit(solution)/shard_map/ppermute | solution.py:20
  22.2 4.1 collective-permute-start.2
  23.3 2.5 copy-start.2
  23.3 3.1 collective-permute-start.3
  41.1 12.9 %copy-start.3 = (bf16[3456,128]{1,0:T(8,128)(2,1)S(1)}, bf16[3456,128]{1,0:T(8,128)(2,1)}, u32[]{:S(2)}) copy-start(bf16[3456,128]{1,0:T(8,128)(2,1)} %get-tuple-element.165) | copy-start | bytes 2654212 | tf_op jit(solution)/shard_map/while
  63.9 12.9 %copy-start.3 = (bf16[3456,128]{1,0:T(8,128)(2,1)S(1)}, bf16[3456,128]{1,0:T(8,128)(2,1)}, u32[]{:S(2)}) copy-start(bf16[3456,128]{1,0:T(8,128)(2,1)} %get-tuple-element.165) | copy-start | bytes 2654212 | tf_op jit(solution)/shard_map/while
  86.7 12.9 %copy-start.3 = (bf16[3456,128]{1,0:T(8,128)(2,1)S(1)}, bf16[3456,128]{1,0:T(8,128)(2,1)}, u32[]{:S(2)}) copy-start(bf16[3456,128]{1,0:T(8,128)(2,1)} %get-tuple-element.165) | copy-start | bytes 2654212 | tf_op jit(solution)/shard_map/while
  109.5 12.9 %copy-start.3 = (bf16[3456,128]{1,0:T(8,128)(2,1)S(1)}, bf16[3456,128]{1,0:T(8,128)(2,1)}, u32[]{:S(2)}) copy-start(bf16[3456,128]{1,0:T(8,128)(2,1)} %get-tuple-element.165) | copy-start | bytes 2654212 | tf_op jit(solution)/shard_map/while
  132.3 12.9 %copy-start.3 = (bf16[3456,128]{1,0:T(8,128)(2,1)S(1)}, bf16[3456,128]{1,0:T(8,128)(2,1)}, u32[]{:S(2)}) copy-start(bf16[3456,128]{1,0:T(8,128)(2,1)} %get-tuple-element.165) | copy-start | bytes 2654212 | tf_op jit(solution)/shard_map/while
  155.1 12.9 %copy-start.3 = (bf16[3456,128]{1,0:T(8,128)(2,1)S(1)}, bf16[3456,128]{1,0:T(8,128)(2,1)}, u32[]{:S(2)}) copy-start(bf16[3456,128]{1,0:T(8,128)(2,1)} %get-tuple-element.165) | copy-start | bytes 2654212 | tf_op jit(solution)/shard_map/while
  177.9 12.9 %copy-start.3 = (bf16[3456,128]{1,0:T(8,128)(2,1)S(1)}, bf16[3456,128]{1,0:T(8,128)(2,1)}, u32[]{:S(2)}) copy-start(bf16[3456,128]{1,0:T(8,128)(2,1)} %get-tuple-element.165) | copy-start | bytes 2654212 | tf_op jit(solution)/shard_map/while
  200.7 12.9 %copy-start.3 = (bf16[3456,128]{1,0:T(8,128)(2,1)S(1)}, bf16[3456,128]{1,0:T(8,128)(2,1)}, u32[]{:S(2)}) copy-start(bf16[3456,128]{1,0:T(8,128)(2,1)} %get-tuple-element.165) | copy-start | bytes 2654212 | tf_op jit(solution)/shard_map/while
  223.5 12.9 %copy-start.3 = (bf16[3456,128]{1,0:T(8,128)(2,1)S(1)}, bf16[3456,128]{1,0:T(8,128)(2,1)}, u32[]{:S(2)}) copy-start(bf16[3456,128]{1,0:T(8,128)(2,1)} %get-tuple-element.165) | copy-start | bytes 2654212 | tf_op jit(solution)/shard_map/while
  246.3 12.9 %copy-start.3 = (bf16[3456,128]{1,0:T(8,128)(2,1)S(1)}, bf16[3456,128]{1,0:T(8,128)(2,1)}, u32[]{:S(2)}) copy-start(bf16[3456,128]{1,0:T(8,128)(2,1)} %get-tuple-element.165) | copy-start | bytes 2654212 | tf_op jit(solution)/shard_map/while
  269.0 12.9 %copy-start.3 = (bf16[3456,128]{1,0:T(8,128)(2,1)S(1)}, bf16[3456,128]{1,0:T(8,128)(2,1)}, u32[]{:S(2)}) copy-start(bf16[3456,128]{1,0:T(8,128)(2,1)} %get-tuple-element.165) | copy-start | bytes 2654212 | tf_op jit(solution)/shard_map/while
  291.9 12.9 %copy-start.3 = (bf16[3456,128]{1,0:T(8,128)(2,1)S(1)}, bf16[3456,128]{1,0:T(8,128)(2,1)}, u32[]{:S(2)}) copy-start(bf16[3456,128]{1,0:T(8,128)(2,1)} %get-tuple-element.165) | copy-start | bytes 2654212 | tf_op jit(solution)/shard_map/while
  314.7 12.9 %copy-start.3 = (bf16[3456,128]{1,0:T(8,128)(2,1)S(1)}, bf16[3456,128]{1,0:T(8,128)(2,1)}, u32[]{:S(2)}) copy-start(bf16[3456,128]{1,0:T(8,128)(2,1)} %get-tuple-element.165) | copy-start | bytes 2654212 | tf_op jit(solution)/shard_map/while
  337.5 12.9 %copy-start.3 = (bf16[3456,128]{1,0:T(8,128)(2,1)S(1)}, bf16[3456,128]{1,0:T(8,128)(2,1)}, u32[]{:S(2)}) copy-start(bf16[3456,128]{1,0:T(8,128)(2,1)} %get-tuple-element.165) | copy-start | bytes 2654212 | tf_op jit(solution)/shard_map/while
  360.3 12.9 %copy-start.3 = (bf16[3456,128]{1,0:T(8,128)(2,1)S(1)}, bf16[3456,128]{1,0:T(8,128)(2,1)}, u32[]{:S(2)}) copy-start(bf16[3456,128]{1,0:T(8,128)(2,1)} %get-tuple-element.165) | copy-start | bytes 2654212 | tf_op jit(solution)/shard_map/while
  383.1 12.9 %copy-start.3 = (bf16[3456,128]{1,0:T(8,128)(2,1)S(1)}, bf16[3456,128]{1,0:T(8,128)(2,1)}, u32[]{:S(2)}) copy-start(bf16[3456,128]{1,0:T(8,128)(2,1)} %get-tuple-element.165) | copy-start | bytes 2654212 | tf_op jit(solution)/shard_map/while
  399.2 115.7 %reduce-scatter.5.cloned.1.call-start = ((), (), s32[]{:S(2)}) async-start(), calls=%async_computation.3 | async-start | bytes 4456448 | tf_op jit(solution)/shard_map/reduce_scatter | solution.py:75
  (1 other events, 1.1 us)
Sparse Core Ops, SparseCore 0:
  399.3 16.6 reduce-scatter.2
  418.3 96.5 reduce-scatter.4
where the time goes:
time: 523 us; the launch traced here: 522 us
  other arithmetic  300 us (57%)
  waiting for transfers between devices  123 us (24%)
  local copies, waits for them, and re-layouts  34.7 us (7%)
  matrix products  33.3 us (6%)
  between operations  13.5 us (3%)
  loops' own time  10.2 us (2%)
  starting transfers between devices  7.2 us (1%)
    convert_element_type x16, other arithmetic, block_term(): adv = adv.astype(jnp.bfloat16).reshape(points * 3, k_count * M)  206 us
    reduce_scatter x1, waiting for transfers between devices, per_device(): owned = lax.psum_scatter(slab, 'gx', scatter_dimension=1, tiled=True)  98.8 us
    convert_element_type x32, other arithmetic, block_term(): part[:, :, :, None].astype(jnp.float32)  68.9 us
    dot_general x16, matrix products, block_term(): lax.dot_general(left, adv, (((0,), (0,)), ((), ())), preferred_element_ty...  33.3 us
    convert_element_type x16, other arithmetic, block_term(): adv = adv + part[:, :, :, None].astype(jnp.float32) * flat[:, comp, None,...  20.2 us
    reduce_scatter x1, waiting for transfers between devices, per_device(): slab = lax.psum_scatter(whole, 'gz', scatter_dimension=0, tiled=True)  16.8 us
    dynamic_update_slice x32, local copies, waits for them, and re-layouts, per_device(): pieces = lax.map(one, jnp.arange(M // step_size, dtype=jnp.int32))  16.7 us
  transfers between devices with their start and end apart: 6, of which 4 were waited for; matrix products, arithmetic and copies ran while one was open for 1% of the time, Pallas kernels for 0%

commit v1 on v0

v1 whole, which is shorter than its diff:
```python
import functools
import math

import jax
import jax.numpy as jnp
from jax import lax
from jax.experimental import pallas as pl
from jax.experimental.pallas import tpu as pltpu
from jax.sharding import PartitionSpec as P

HALO = 3
TILE = 256
WIDE = 128
MODES_OF = ("b", "b", "f")
COEFS = (0.75, -0.15, 1.0 / 60.0)


def ring(count, step):
    return [(i, (i + step) % count) for i in range(count)]


def prep_kernel(xs, planes, zs, gran, scal_ref, m_ref, w_ref, gb_ref, gf_ref, mt_ref, wn_ref, tmp_ref):
    t = pl.program_id(0)
    xor = scal_ref[0]
    row0 = pl.multiple_of(scal_ref[1], 8)
    rows = planes * zs
    comps, _, modes = wn_ref.shape[1:]
    modes //= 2
    keep = mt_ref.shape[2]
    gx, gy, gz, own = [], [], [], []
    for xi in range(xs):
        base = t * xs + xi + HALO
        mid = m_ref[base]
        total = jnp.zeros(mid.shape, jnp.float32)
        for shift, coef in zip((1, 2, 3), COEFS):
            upper = m_ref[base + shift].astype(jnp.float32)
            lower = m_ref[base - shift].astype(jnp.float32)
            total = total + coef * (upper - lower)
        gx.append(total)
        f = mid.astype(jnp.float32)
        parts = []
        for plane in range(planes):
            g = f[plane * zs : (plane + 1) * zs]
            total = jnp.zeros(g.shape, jnp.float32)
            for shift, coef in zip((1, 2, 3), COEFS):
                total = total + coef * (pltpu.roll(g, zs - shift, 0) - pltpu.roll(g, shift, 0))
            parts.append(total)
        gz.append(jnp.concatenate(parts, 0))
        gy.append(w_ref[t * xs + xi].astype(jnp.float32))
        own.append(f)
    grads = [jnp.concatenate(g, 0) for g in (gx, gy, gz)]
    flat = jnp.concatenate(own, 0)
    zero = jnp.zeros((xs * rows, modes), jnp.bfloat16)
    ib = jf = 0
    for c in range(comps):
        cols = slice(c * modes, (c + 1) * modes)
        wn_ref[0, c, :, 0:modes] = flat[:, cols].astype(jnp.bfloat16)
        wn_ref[0, c, :, modes : 2 * modes] = zero
        tmp_ref[...] = flat[:, cols].T
        mt_ref[0, c] = tmp_ref[pl.ds(row0, keep), :]
        for a in range(3):
            g = grads[a][:, cols].astype(jnp.bfloat16).astype(jnp.float32)
            tmp_ref[...] = g.T
            for b in range(modes // gran):
                src = pl.multiple_of((b ^ xor) * gran, 8)
                v = tmp_ref[pl.ds(src, gran), :]
                if MODES_OF[c] == "b":
                    gb_ref[0, ib, b * gran : (b + 1) * gran, :] = v.astype(jnp.bfloat16)
                else:
                    gf_ref[0, jf, b * gran : (b + 1) * gran, :] = v
            if MODES_OF[c] == "b":
                ib += 1
            else:
                jf += 1


def prepare(mfull, wfull, xor, row0, keep, modes, gran):
    cells, planes, zs, comps_modes = wfull.shape
    comps = comps_modes // modes
    rows = planes * zs
    xs = WIDE // math.gcd(rows, WIDE)
    points = cells * rows
    step = xs * rows
    wide = TILE * math.gcd(points // TILE, 9)
    chunks, steps = points // wide, wide // step
    nb, nf = MODES_OF.count("b"), MODES_OF.count("f")
    scal = jnp.stack([xor, row0]).astype(jnp.int32)
    return pl.pallas_call(
        functools.partial(prep_kernel, xs, planes, zs, gran),
        grid_spec=pltpu.PrefetchScalarGridSpec(
            num_scalar_prefetch=1,
            grid=(cells // xs,),
            in_specs=[
                pl.BlockSpec((cells + 2 * HALO, rows, comps_modes), lambda t, s: (0, 0, 0), pipeline_mode=pl.Buffered(1)),
                pl.BlockSpec((cells, rows, comps_modes), lambda t, s: (0, 0, 0), pipeline_mode=pl.Buffered(1)),
            ],
            out_specs=[
                pl.BlockSpec((1, 3 * nb, modes, step), lambda t, s: (t // steps, 0, 0, t % steps)),
                pl.BlockSpec((1, 3 * nf, modes, step), lambda t, s: (t // steps, 0, 0, t % steps)),
                pl.BlockSpec((1, comps, keep, step), lambda t, s: (t // steps, 0, 0, t % steps)),
                pl.BlockSpec((1, comps, step, 2 * modes), lambda t, s: (t // steps, 0, t % steps, 0)),
            ],
            scratch_shapes=[pltpu.VMEM((modes, step), jnp.float32)],
        ),
        out_shape=[
            jax.ShapeDtypeStruct((chunks, 3 * nb, modes, wide), jnp.bfloat16),
            jax.ShapeDtypeStruct((chunks, 3 * nf, modes, wide), jnp.float32),
            jax.ShapeDtypeStruct((chunks, comps, keep, wide), jnp.float32),
            jax.ShapeDtypeStruct((chunks, comps, wide, 2 * modes), jnp.bfloat16),
        ],
        compiler_params=pltpu.CompilerParams(vmem_limit_bytes=28 << 20),
        name="prep",
    )(scal, mfull.reshape(cells + 2 * HALO, rows, comps_modes), wfull.reshape(cells, rows, comps_modes))


def tensor_kernel(jobs, gran, gb_ref, gf_ref, mt_ref, wn_ref, *outs):
    chunks, _, _, wide = mt_ref.shape
    modes = wn_ref.shape[3] // 2
    for (j_from, j_count, blocks), o_ref in zip(jobs, outs):
        rows = len(blocks) * gran
        per = min(TILE // rows if rows < TILE else 1, j_count // 2)
        group = 2 * per

        def step(t, _, j_from=j_from, blocks=blocks, o_ref=o_ref, rows=rows, per=per, group=group):
            j0 = j_from + t * group

            def scoped(*accs):
                def tiles(n):
                    stage = 0
                    for pt in range(wide // TILE):
                        cols = pl.ds(pt * TILE, TILE)
                        ib = jf = 0
                        for c, kind in enumerate(MODES_OF):
                            w = wn_ref[n, c, cols, :]
                            for x in range(2):
                                pltpu.matmul_push_rhs(w, stage, x)
                            for q in range(per):
                                ms = []
                                for x in range(2):
                                    j = j0 + x * per + q
                                    m = [jnp.broadcast_to(mt_ref[n, a, pl.ds(j, 1), cols], (8, TILE)) for a in range(3)]
                                    if kind == "b":
                                        m = [v.astype(jnp.bfloat16) for v in m]
                                    ms.append(m)
                                vals = ([], [])
                                for b in blocks:
                                    for h in range(gran // 8):
                                        ks = pl.ds(b * gran + h * 8, 8)
                                        if kind == "b":
                                            g = [gb_ref[n, ib + a, ks, cols] for a in range(3)]
                                        else:
                                            g = [gf_ref[n, jf + a, ks, cols] for a in range(3)]
                                        for x in range(2):
                                            m = ms[x]
                                            vals[x].append(m[0] * g[0] + m[1] * g[1] + m[2] * g[2])
                                for x in range(2):
                                    lhs = jnp.concatenate(vals[x], 0).astype(jnp.bfloat16)
                                    pltpu.matmul_acc_lhs(
                                        accs[x * per + q], lhs, load_staged_rhs=stage if q == 0 else None
                                    )
                            stage ^= 1
                            if kind == "b":
                                ib += 3
                            else:
                                jf += 3

                if chunks == 1:
                    tiles(0)
                else:
                    lax.fori_loop(0, chunks, lambda n, _: (tiles(n), 0)[1], 0)
                for x in range(2):
                    for q in range(per):
                        full = pltpu.matmul_pop(accs[x * per + q])
                        o_ref[t * group + x * per + q] = full[:, :modes].astype(o_ref.dtype)

            pl.run_scoped(scoped, *[pltpu.ACC(x)((rows, TILE), jnp.float32) for x in range(2) for _ in range(per)])
            return 0

        lax.fori_loop(0, j_count // group, step, 0)


def tensor(jobs, gran, dtype, gb, gf, mt, wn, name):
    modes = wn.shape[3] // 2
    rows = sum(j_count * len(blocks) * gran for _, j_count, blocks in jobs)
    return pl.pallas_call(
        functools.partial(tensor_kernel, jobs, gran),
        in_specs=[pl.BlockSpec(memory_space=pltpu.VMEM)] * 4,
        out_specs=[pl.BlockSpec(memory_space=pltpu.VMEM)] * len(jobs),
        out_shape=[
            jax.ShapeDtypeStruct((j_count, len(blocks) * gran, modes), dtype) for _, j_count, blocks in jobs
        ],
        compiler_params=pltpu.CompilerParams(vmem_limit_bytes=24 << 20),
        cost_estimate=pl.CostEstimate(
            flops=2 * rows * mt.shape[1] * mt.shape[0] * mt.shape[3] * modes, bytes_accessed=16 << 20, transcendentals=0
        ),
        name=name,
    )(gb, gf, mt, wn)


def ordered(bits):
    if not bits:
        return [0]
    rest = ordered(bits[1:])
    return [b | bits[0] for b in rest] + rest


def per_device(modes, wall_grad):
    planes, cells_x, cells_z, comps, m = modes.shape
    count_x, count_z = lax.axis_size("gx"), lax.axis_size("gz")
    weight = 1.0 / math.sqrt(planes * cells_x * cells_z * count_x * count_z)
    me, mez = lax.axis_index("gx"), lax.axis_index("gz")
    own = jnp.transpose(modes.reshape(planes, cells_x, cells_z, comps * m), (1, 0, 2, 3))
    wall = jnp.transpose(wall_grad.reshape(planes, cells_x, cells_z, comps * m), (1, 0, 2, 3))
    low = lax.ppermute(own[cells_x - HALO :], "gx", ring(count_x, 1))
    high = lax.ppermute(own[:HALO], "gx", ring(count_x, -1))

    def around(block):
        return [block] + [lax.ppermute(block, "gz", ring(count_z, -s)) for s in range(1, count_z)]

    both = around(jnp.concatenate([own, wall], 0))
    halos = around(jnp.concatenate([low, high], 0))
    mfull = jnp.concatenate(
        [
            jnp.concatenate([h[:HALO] for h in halos], 2),
            jnp.concatenate([b[:cells_x] for b in both], 2),
            jnp.concatenate([h[HALO:] for h in halos], 2),
        ],
        0,
    )
    wfull = jnp.concatenate([b[cells_x:] for b in both], 2)

    slab = m // count_x
    gran = max(8, slab)
    inner = gran // slab
    keep = m // count_z
    operands = prepare(mfull, wfull, me // inner, mez * keep, keep, m, gran)

    bits = [1 << s for s in range((m // gran).bit_length() - 1)]
    order = ordered(bits)
    half = len(order) // 2
    quarter = half // 2
    pieces = (order[:half], order[half : half + quarter], order[half + quarter :])

    def swap(block, bit):
        return lax.ppermute(block.astype(jnp.bfloat16), "gx", [(i, i ^ bit) for i in range(count_x)])

    (first,) = tensor([(0, keep, pieces[0])], gran, jnp.bfloat16, *operands, "first")
    got = swap(first, bits[0] * inner)
    (second,) = tensor([(0, keep, pieces[1])], gran, jnp.float32, *operands, "second")
    (third,) = tensor([(0, keep, pieces[2])], gran, jnp.float32, *operands, "third")
    cut = quarter * gran
    got2 = swap(second + got[:, :cut].astype(jnp.float32), bits[1] * inner)
    rest = third + got[:, cut:].astype(jnp.float32) + got2.astype(jnp.float32)
    for bit in bits[2:]:
        cut = rest.shape[1] // 2
        got = swap(rest[:, :cut], bit * inner)
        rest = rest[:, cut:] + got.astype(jnp.float32)
    bit = inner // 2
    while bit:
        cut = rest.shape[1] // 2
        upper = (me & bit) != 0
        send = jnp.where(upper, rest[:, :cut], rest[:, cut:])
        stay = jnp.where(upper, rest[:, cut:], rest[:, :cut])
        rest = stay + swap(send, bit).astype(jnp.float32)
        bit //= 2
    turned = jnp.transpose(rest, (1, 2, 0)) * weight
    return lax.all_to_all(turned, "gz", 1, 2, tiled=True)


def solution(mesh):
    placed = (P(None, "gx", "gz", None, None), P(None, "gx", "gz", None, None))
    return jax.shard_map(
        per_device, mesh=mesh, in_specs=placed, out_specs=P("gx", "gz", None), check_vma=False
    )
```

time: 523 us -> 123 us (0.24)
  other arithmetic: 300 us -> 4.75 us
  waiting for transfers between devices: 123 us -> 31.7 us
  Pallas kernels: 0 us -> 60.3 us
  matrix products: 33.3 us -> 0 us
  local copies, waits for them, and re-layouts: 34.7 us -> 7.88 us
  between operations: 13.5 us -> 0.17 us
  loops' own time: 10.2 us -> 0 us
  starting transfers between devices: 7.2 us -> 14.1 us
    convert_element_type x66 -> x1, other arithmetic: 300 us -> 0.17 us  [swap(): block.astype(jnp.bfloat16)]
    reduce_scatter x2 -> x0, waiting for transfers between devices: 116 us -> none  [the longest x1 98.8 us: per_device(): owned = lax.psum_scatter(slab, 'gx', scatter_dimension=1, tiled=True)]
    pallas_call x0 -> x4, Pallas kernels: none -> 60.3 us  [the longest x3 51.6 us: tensor(): pl.pallas_call(functools.partial(tensor_kernel, jobs, gran), in_specs=[pl...]
    dot_general x16 -> x0, matrix products: 33.3 us -> none  [block_term(): lax.dot_general(left, adv, (((0,), (0,)), ((), ())), preferred_element_ty...]
    ppermute x4 -> x8, waiting for transfers between devices: 7.16 us -> 31.7 us  [the longest x4 21.8 us: swap(): lax.ppermute(block.astype(jnp.bfloat16), 'gx', [(i, i ^ bit) for i in ran...]
    dynamic_update_slice x32 -> x0, local copies, waits for them, and re-layouts: 16.7 us -> none  [per_device(): pieces = lax.map(one, jnp.arange(M // step_size, dtype=jnp.int32))]
    another operation x1 -> x0, loops' own time: 10.2 us -> none  [per_device(): pieces = lax.map(one, jnp.arange(M // step_size, dtype=jnp.int32))]
    dynamic_slice x16 -> x0, local copies, waits for them, and re-layouts: 9.15 us -> none  [per_device(): pieces = lax.map(one, jnp.arange(M // step_size, dtype=jnp.int32))]
  transfers between devices with their start and end apart: 6 -> 8, of which waited for: 4 -> 6; matrix products, arithmetic and copies ran while one was open for 1% -> 1% of each run, Pallas kernels for 0% -> 21%
where the time goes in v1:
time: 123 us
  Pallas kernels  60.3 us (49%)
  waiting for transfers between devices  31.7 us (26%)
  starting transfers between devices  14.1 us (11%)
  local copies, waits for them, and re-layouts  7.88 us (6%)
  other arithmetic  4.75 us (4%)
  blocking collectives  3.94 us (3%)
    pallas_call x3, Pallas kernels, tensor(): pl.pallas_call(functools.partial(tensor_kernel, jobs, gran), in_specs=[pl...  51.6 us
    ppermute x4, waiting for transfers between devices, swap(): lax.ppermute(block.astype(jnp.bfloat16), 'gx', [(i, i ^ bit) for i in ran...  21.8 us
    pallas_call x1, Pallas kernels, prepare(): pl.pallas_call(functools.partial(prep_kernel, xs, planes, zs, gran), grid...  8.74 us
    ppermute x4, starting transfers between devices, swap(): lax.ppermute(block.astype(jnp.bfloat16), 'gx', [(i, i ^ bit) for i in ran...  6.97 us
    ppermute x1, waiting for transfers between devices, per_device(): low = lax.ppermute(own[cells_x - HALO:], 'gx', ring(count_x, 1))  6.14 us
    ppermute x1, starting transfers between devices, per_device(): high = lax.ppermute(own[:HALO], 'gx', ring(count_x, -1))  4.06 us
    all_to_all x1, blocking collectives, per_device(): return lax.all_to_all(turned, 'gz', 1, 2, tiled=True)  3.94 us
    ppermute x1, starting transfers between devices, per_device(): low = lax.ppermute(own[cells_x - HALO:], 'gx', ring(count_x, 1))  2.53 us
  transfers between devices with their start and end apart: 8, of which 6 were waited for; matrix products, arithmetic and copies ran while one was open for 1% of the time, Pallas kernels for 21%

profile of v1, /device:TPU:0, one launch (start us, length us, event | category | flops | bytes accessed | tf_op | source)
XLA Modules:
  0.0 122.9 jit_solution(2807942601742142683)
XLA Ops:
  0.0 1.2 copy-done
  1.2 1.3 %bitcast_bitcast_fusion = (bf16[12,2,48,384]{3,2,0,1:T(8,128)(2,1)S(1)}, bf16[12,2,48,384]{3,2,0,1:T(8,128)(2,1)S(1)}) fusion(bf16[2,12,48,3,128]{4,2,3,1,0:T(8,128)(2,1)S(1)} %copy-done, bf16[2,12,48,3,128]{4,2,3,1,0:T(8,128)(2,1)} %param.3), kind=kLoop, calls=%fused_computation.5 | loop fusion | bytes 3538944 | tf_op jit(solution)/shard_map/transpose | solution.py:213
  2.5 1.4 %pad_maximum_fusion = bf16[24,2,48,384]{3,2,0,1:T(8,128)(2,1)} fusion(bf16[12,2,48,384]{3,2,0,1:T(8,128)(2,1)S(1)} %get-tuple-element.19, bf16[12,2,48,384]{3,2,0,1:T(8,128)(2,1)S(1)} %get-tuple-element.20), kind=kLoop, calls=%fused_computation.1 | loop fusion | flops 884736 | bytes 3538944 | tf_op jit(solution)/shard_map/concatenate | solution.py:220
  4.5 2.5 %collective-permute-start = (bf16[3,2,48,384]{3,2,0,1:T(8,128)(2,1)S(1)}, bf16[3,2,48,384]{3,2,0,1:T(8,128)(2,1)S(1)}, u32[]{:S(2)}, u32[]{:S(2)}) collective-permute-start(bf16[3,2,48,384]{3,2,0,1:T(8,128)(2,1)S(1)} %get-tuple-element.15), channel_id=1, source_target_pairs={{0,2},{2,4},{4,6},{6,8},{8,10},{10,12},{12,14},{14,16},{16,18},{18... | collective-permute-start | bytes 663560 | tf_op jit(solution)/shard_map/ppermute | solution.py:214
  7.0 4.1 %collective-permute-start.1 = (bf16[3,2,48,384]{3,2,0,1:T(8,128)(2,1)S(1)}, bf16[3,2,48,384]{3,2,0,1:T(8,128)(2,1)S(1)}, u32[]{:S(2)}, u32[]{:S(2)}) collective-permute-start(bf16[3,2,48,384]{3,2,0,1:T(8,128)(2,1)S(1)} %get-tuple-element.16), channel_id=1, source_target_pairs={{0,30},{2,0},{4,2},{6,4},{8,6},{10,8},{12,10},{14,12},{16,14},{18,... | collective-permute-start | bytes 663560 | tf_op jit(solution)/shard_map/ppermute | solution.py:215
  11.1 6.1 %collective-permute-done = bf16[3,2,48,384]{3,2,0,1:T(8,128)(2,1)S(1)} collective-permute-done((bf16[3,2,48,384]{3,2,0,1:T(8,128)(2,1)S(1)}, bf16[3,2,48,384]{3,2,0,1:T(8,128)(2,1)S(1)}, u32[]{:S(2)}, u32[]{:S(2)}) %collective-permute-start) | collective-permute-done | bytes 221216 | tf_op jit(solution)/shard_map/ppermute | solution.py:214
  17.2 1.8 %collective-permute-done.1 = bf16[3,2,48,384]{3,2,0,1:T(8,128)(2,1)S(1)} collective-permute-done((bf16[3,2,48,384]{3,2,0,1:T(8,128)(2,1)S(1)}, bf16[3,2,48,384]{3,2,0,1:T(8,128)(2,1)S(1)}, u32[]{:S(2)}, u32[]{:S(2)}) %collective-permute-start.1) | collective-permute-done | bytes 221216 | tf_op jit(solution)/shard_map/ppermute | solution.py:215
  19.1 0.8 pad_maximum_fusion.2
  20.0 1.9 %collective-permute-done.2 = bf16[6,2,48,384]{3,2,0,1:T(8,128)(2,1)S(1)} collective-permute-done((bf16[6,2,48,384]{3,2,0,1:T(8,128)(2,1)}, bf16[6,2,48,384]{3,2,0,1:T(8,128)(2,1)S(1)}, u32[]{:S(2)}, u32[]{:S(2)}) %collective-permute-start.2) | collective-permute-done | bytes 442400 | tf_op jit(solution)/shard_map/ppermute | solution.py:218
  22.0 1.6 %fusion.2 = (bf16[12,2,48,384]{3,2,0,1:T(8,128)(2,1)S(1)}, bf16[12,2,48,384]{3,2,0,1:T(8,128)(2,1)S(1)}) fusion(bf16[24,2,48,384]{3,2,0,1:T(8,128)(2,1)} %collective-permute-done.3), kind=kLoop, calls=%fused_computation.15 | loop fusion | bytes 3538944 | tf_op jit(solution)/shard_map/slice | solution.py:230
  24.8 8.7 %prep.1 = (bf16[1,6,128,2304]{3,2,1,0:T(8,128)(2,1)S(1)}, f32[1,3,128,2304]{3,2,1,0:T(8,128)S(1)}, f32[1,3,64,2304]{3,2,1,0:T(8,128)S(1)}, bf16[1,3,2304,256]{3,2,1,0:T(8,128)(2,1)S(1)}) custom-call(s32[2]{0:T(128)S(1)} %pad_add_fusion.scal_ref, bf16[18,192,384]{2,1,0:T(8,128)(2,1)S(1)} %bitcast.25, bf16[12,192,384]{2,1,0:T(8,128)(2,1)S(1)} %bitcast.26), custom_call_target="tpu_custom_call" | custom-call | tf_op jit(solution)/shard_map/prep/pallas_call | solution.py:88
  33.6 25.8 %first.1 = bf16[64,64,128]{2,1,0:T(8,128)(2,1)S(1)} custom-call(bf16[1,6,128,2304]{3,2,1,0:T(8,128)(2,1)S(1)} %get-tuple-element.9.gb_ref, f32[1,3,128,2304]{3,2,1,0:T(8,128)S(1)} %get-tuple-element.10.gf_ref, f32[1,3,64,2304]{3,2,1,0:T(8,128)S(1)} %get-tuple-element.11.mt_ref, bf16[1,3,2304,256]{3,2,1,0:T(8,128)(2,1)S(1)} %get-tuple-element.12.wn_ref), custom_call_target="tpu_custom_call" | custom-call | flops 7247757312 | bytes 16777216 | tf_op jit(solution)/shard_map/first/pallas_call | solution.py:185
  59.4 1.6 %collective-permute-start.4 = (bf16[64,64,128]{2,1,0:T(8,128)(2,1)S(1)}, bf16[64,64,128]{2,1,0:T(8,128)(2,1)S(1)}, u32[]{:S(2)}, u32[]{:S(2)}) collective-permute-start(bf16[64,64,128]{2,1,0:T(8,128)(2,1)S(1)} %first.1), channel_id=1, source_target_pairs={{0,2},{2,0},{4,6},{6,4},{8,10},{10,8},{12,14},{14,12},{16,18},{18,... | collective-permute-start | bytes 3145736 | tf_op jit(solution)/shard_map/ppermute | solution.py:245
  61.0 12.9 %second.1 = f32[64,32,128]{2,1,0:T(8,128)S(1)} custom-call(bf16[1,6,128,2304]{3,2,1,0:T(8,128)(2,1)S(1)} %get-tuple-element.9.gb_ref, f32[1,3,128,2304]{3,2,1,0:T(8,128)S(1)} %get-tuple-element.10.gf_ref, f32[1,3,64,2304]{3,2,1,0:T(8,128)S(1)} %get-tuple-element.11.mt_ref, bf16[1,3,2304,256]{3,2,1,0:T(8,128)(2,1)S(1)} %get-tuple-element.12.wn_ref), custom_call_target="tpu_custom_call" | custom-call | flops 3623878656 | bytes 16777216 | tf_op jit(solution)/shard_map/second/pallas_call | solution.py:185
  73.9 10.8 %collective-permute-done.4 = bf16[64,64,128]{2,1,0:T(8,128)(2,1)S(1)} collective-permute-done((bf16[64,64,128]{2,1,0:T(8,128)(2,1)S(1)}, bf16[64,64,128]{2,1,0:T(8,128)(2,1)S(1)}, u32[]{:S(2)}, u32[]{:S(2)}) %collective-permute-start.4) | collective-permute-done | bytes 1048608 | tf_op jit(solution)/shard_map/ppermute | solution.py:245
  84.8 1.8 %collective-permute-start.5 = (bf16[64,32,128]{2,1,0:T(8,128)(2,1)S(1)}, bf16[64,32,128]{2,1,0:T(8,128)(2,1)S(1)}, u32[]{:S(2)}, u32[]{:S(2)}) collective-permute-start(bf16[64,32,128]{2,1,0:T(8,128)(2,1)S(1)} %add_convert_fusion), channel_id=1, source_target_pairs={{0,4},{2,6},{4,0},{6,2},{8,12},{10,14},{12,8},{14,10},{16,20},{18,... | collective-permute-start | bytes 1572872 | tf_op jit(solution)/shard_map/ppermute | solution.py:245
  86.7 12.9 %third.1 = f32[64,32,128]{2,1,0:T(8,128)S(1)} custom-call(bf16[1,6,128,2304]{3,2,1,0:T(8,128)(2,1)S(1)} %get-tuple-element.9.gb_ref, f32[1,3,128,2304]{3,2,1,0:T(8,128)S(1)} %get-tuple-element.10.gf_ref, f32[1,3,64,2304]{3,2,1,0:T(8,128)S(1)} %get-tuple-element.11.mt_ref, bf16[1,3,2304,256]{3,2,1,0:T(8,128)(2,1)S(1)} %get-tuple-element.12.wn_ref), custom_call_target="tpu_custom_call" | custom-call | flops 3623878656 | bytes 16777216 | tf_op jit(solution)/shard_map/third/pallas_call | solution.py:185
  99.8 1.3 %collective-permute-start.6 = (bf16[64,16,128]{2,1,0:T(8,128)(2,1)S(1)}, bf16[64,16,128]{2,1,0:T(8,128)(2,1)S(1)}, u32[]{:S(2)}, u32[]{:S(2)}) collective-permute-start(bf16[64,16,128]{2,1,0:T(8,128)(2,1)S(1)} %slice.72), channel_id=1, source_target_pairs={{0,8},{2,10},{4,12},{6,14},{8,0},{10,2},{12,4},{14,6},{16,24},{18,... | collective-permute-start | bytes 786440 | tf_op jit(solution)/shard_map/ppermute | solution.py:245
  101.1 6.0 %collective-permute-done.6 = bf16[64,16,128]{2,1,0:T(8,128)(2,1)S(1)} collective-permute-done((bf16[64,16,128]{2,1,0:T(8,128)(2,1)S(1)}, bf16[64,16,128]{2,1,0:T(8,128)(2,1)S(1)}, u32[]{:S(2)}, u32[]{:S(2)}) %collective-permute-start.6) | collective-permute-done | bytes 262176 | tf_op jit(solution)/shard_map/ppermute | solution.py:245
  107.2 2.3 %collective-permute-start.7 = (bf16[64,8,128]{2,1,0:T(8,128)(2,1)S(1)}, bf16[64,8,128]{2,1,0:T(8,128)(2,1)S(1)}, u32[]{:S(2)}, u32[]{:S(2)}) collective-permute-start(bf16[64,8,128]{2,1,0:T(8,128)(2,1)S(1)} %slice.73), channel_id=1, source_target_pairs={{0,16},{2,18},{4,20},{6,22},{8,24},{10,26},{12,28},{14,30},{16,0},... | collective-permute-start | bytes 393224 | tf_op jit(solution)/shard_map/ppermute | solution.py:245
  109.5 5.0 %collective-permute-done.7 = bf16[64,8,128]{2,1,0:T(8,128)(2,1)S(1)} collective-permute-done((bf16[64,8,128]{2,1,0:T(8,128)(2,1)S(1)}, bf16[64,8,128]{2,1,0:T(8,128)(2,1)S(1)}, u32[]{:S(2)}, u32[]{:S(2)}) %collective-permute-start.7) | collective-permute-done | bytes 131104 | tf_op jit(solution)/shard_map/ppermute | solution.py:245
  115.2 3.9 %all_to_all.18 = f32[2,1,32768]{2,1,0:T(1,128)S(1)} all-to-all(f32[2,1,32768]{2,1,0:T(1,128)S(1)} %reshape.16), channel_id=1, replica_groups=mesh['gx'=16,'gz'=2] {'gz'}, dimensions={0} | all-to-all | bytes 524288 | tf_op jit(solution)/shard_map/all_to_all | solution.py:267
  119.6 1.4 %reduce = f32[2,32768]{1,0:T(2,128)S(1)} reduce(f32[2,1,32768]{2,1,0:T(1,128)S(1)} %all_to_all.18, f32[]{:T(128)} %broadcast.3), dimensions={1}, to_apply=%all_to_all.13.reduce_sub_computation | reduce | bytes 524292 | tf_op jit(solution)/shard_map/all_to_all | solution.py:267
  121.8 1.0 all_to_all.16
  (23 shorter events, 4.3 us)
Async XLA Ops:
  0.0 1.2 copy-start
  3.9 18.0 %collective-permute-start.3 = (bf16[24,2,48,384]{3,2,0,1:T(8,128)(2,1)}, bf16[24,2,48,384]{3,2,0,1:T(8,128)(2,1)}, u32[]{:S(2)}, u32[]{:S(2)}) collective-permute-start(bf16[24,2,48,384]{3,2,0,1:T(8,128)(2,1)} %pad_maximum_fusion), channel_id=1, source_target_pairs={{0,1},{1,0},{2,3},{3,2},{4,5},{5,4},{6,7},{7,6},{8,9},{9,8},{10,11... | collective-permute-start | bytes 5308424 | tf_op jit(solution)/shard_map/ppermute | solution.py:218
  4.5 12.7 %collective-permute-start = (bf16[3,2,48,384]{3,2,0,1:T(8,128)(2,1)S(1)}, bf16[3,2,48,384]{3,2,0,1:T(8,128)(2,1)S(1)}, u32[]{:S(2)}, u32[]{:S(2)}) collective-permute-start(bf16[3,2,48,384]{3,2,0,1:T(8,128)(2,1)S(1)} %get-tuple-element.15), channel_id=1, source_target_pairs={{0,2},{2,4},{4,6},{6,8},{8,10},{10,12},{12,14},{14,16},{16,18},{18... | collective-permute-start | bytes 663560 | tf_op jit(solution)/shard_map/ppermute | solution.py:214
  7.0 12.0 %collective-permute-start.1 = (bf16[3,2,48,384]{3,2,0,1:T(8,128)(2,1)S(1)}, bf16[3,2,48,384]{3,2,0,1:T(8,128)(2,1)S(1)}, u32[]{:S(2)}, u32[]{:S(2)}) collective-permute-start(bf16[3,2,48,384]{3,2,0,1:T(8,128)(2,1)S(1)} %get-tuple-element.16), channel_id=1, source_target_pairs={{0,30},{2,0},{4,2},{6,4},{8,6},{10,8},{12,10},{14,12},{16,14},{18,... | collective-permute-start | bytes 663560 | tf_op jit(solution)/shard_map/ppermute | solution.py:215
  19.9 2.0 %collective-permute-start.2 = (bf16[6,2,48,384]{3,2,0,1:T(8,128)(2,1)}, bf16[6,2,48,384]{3,2,0,1:T(8,128)(2,1)S(1)}, u32[]{:S(2)}, u32[]{:S(2)}) collective-permute-start(bf16[6,2,48,384]{3,2,0,1:T(8,128)(2,1)} %pad_maximum_fusion.2), channel_id=1, source_target_pairs={{0,1},{1,0},{2,3},{3,2},{4,5},{5,4},{6,7},{7,6},{8,9},{9,8},{10,11... | collective-permute-start | bytes 1327112 | tf_op jit(solution)/shard_map/ppermute | solution.py:218
  59.4 25.3 %collective-permute-start.4 = (bf16[64,64,128]{2,1,0:T(8,128)(2,1)S(1)}, bf16[64,64,128]{2,1,0:T(8,128)(2,1)S(1)}, u32[]{:S(2)}, u32[]{:S(2)}) collective-permute-start(bf16[64,64,128]{2,1,0:T(8,128)(2,1)S(1)} %first.1), channel_id=1, source_target_pairs={{0,2},{2,0},{4,6},{6,4},{8,10},{10,8},{12,14},{14,12},{16,18},{18,... | collective-permute-start | bytes 3145736 | tf_op jit(solution)/shard_map/ppermute | solution.py:245
  84.8 14.7 %collective-permute-start.5 = (bf16[64,32,128]{2,1,0:T(8,128)(2,1)S(1)}, bf16[64,32,128]{2,1,0:T(8,128)(2,1)S(1)}, u32[]{:S(2)}, u32[]{:S(2)}) collective-permute-start(bf16[64,32,128]{2,1,0:T(8,128)(2,1)S(1)} %add_convert_fusion), channel_id=1, source_target_pairs={{0,4},{2,6},{4,0},{6,2},{8,12},{10,14},{12,8},{14,10},{16,20},{18,... | collective-permute-start | bytes 1572872 | tf_op jit(solution)/shard_map/ppermute | solution.py:245
  99.8 7.3 %collective-permute-start.6 = (bf16[64,16,128]{2,1,0:T(8,128)(2,1)S(1)}, bf16[64,16,128]{2,1,0:T(8,128)(2,1)S(1)}, u32[]{:S(2)}, u32[]{:S(2)}) collective-permute-start(bf16[64,16,128]{2,1,0:T(8,128)(2,1)S(1)} %slice.72), channel_id=1, source_target_pairs={{0,8},{2,10},{4,12},{6,14},{8,0},{10,2},{12,4},{14,6},{16,24},{18,... | collective-permute-start | bytes 786440 | tf_op jit(solution)/shard_map/ppermute | solution.py:245
  107.2 7.3 %collective-permute-start.7 = (bf16[64,8,128]{2,1,0:T(8,128)(2,1)S(1)}, bf16[64,8,128]{2,1,0:T(8,128)(2,1)S(1)}, u32[]{:S(2)}, u32[]{:S(2)}) collective-permute-start(bf16[64,8,128]{2,1,0:T(8,128)(2,1)S(1)} %slice.73), channel_id=1, source_target_pairs={{0,16},{2,18},{4,20},{6,22},{8,24},{10,26},{12,28},{14,30},{16,0},... | collective-permute-start | bytes 393224 | tf_op jit(solution)/shard_map/ppermute | solution.py:245
